TPU v7x, 256 devices: a whole 4x4x8 slice. The times are simulated.
256 devices in a mesh: grid: 128 (over x, z, y), rep: 2 (over core).
Axes of the slice: x: 4, y: 4, z: 8, core: 2. Of those that a mesh axis runs over, the one named last changes fastest.
Arguments:
- density_blocks: bfloat16 [3584, 4, 128, 128], P('grid'), may hold values from -0.046875 to 0.046875
- neighbours: int32 [3584, 4], P('grid'), may hold values from 0 to 3583, as said below
- relevant: int32 [3072, 8], P(('grid', 'rep')), may hold values from 0 to 3583, as said below
- batch_count: int32 [256], P(('grid', 'rep')), may hold values from 1 to 12, as said below
- basis_values: bfloat16 [3072, 8, 128, 128], P(('grid', 'rep')), may hold values from -6 to 6
- becke_weights: bfloat16 [3072, 128], P(('grid', 'rep')), may hold values from 0.0039978027 to 0.099609375
Outputs:
- xc_blocks: bfloat16 [3584, 4, 128, 128], P('grid')
Inputs may be any that keep to these rules, and one draw needn't show every extreme that they name: neighbours[a, 0] = a; the 4 column groups of a row group are distinct and lie within 12 consecutive groups that contain a. `relevant`: the 8 groups of a batch are distinct and lie within 12 consecutive groups around a group owned by the batch's grid index; none lies more than 6 groups before the first or after the last group owned by that grid index. `batch_count`: some device has all 12 slots live in every draw.
All inputs are finite; a program needn't handle non-finite values.
Results may differ from a plain program's by a relative error of at most 0.0049.
Values may be sent and summed in bfloat16 or wider, within the bound.
A program may use at most 192 MiB of HBM per device.

v0:
```python
import jax
import jax.numpy as jnp
from jax import lax
from jax.sharding import PartitionSpec as P

SPAN = 12
slater_coef = 0.9847450218426965


def shifted(block, axis, distance):
    devices = range(lax.axis_size(axis))
    route = [(i - distance, i) for i in devices if i - distance in devices]
    return lax.ppermute(block, axis, route)


def in_blocks(array, dim, count):
    before, after = (array.shape[:dim], array.shape[dim + 1 :])
    return jnp.moveaxis(array.reshape(*before, count, -1, *after), dim, 0)


def sum_at_owner(array, axis, dim):
    count = lax.axis_size(axis)
    pieces = lax.all_to_all(in_blocks(array, dim, count), axis, 0, 0, tiled=True)
    return jnp.sum(pieces, axis=0)


def potential(density_at):
    return -slater_coef * density_at * (density_at * density_at + 1.0) ** (-1.0 / 3.0)


def batch_terms(slabs, slab_neighbours, groups, basis_vals, weight_row):
    matches = (slab_neighbours[:, :, None] == groups[None, None, :]).astype(jnp.bfloat16)
    column_basis = jnp.einsum(
        "ikj,jnp->iknp", matches, basis_vals, preferred_element_type=jnp.float32
    ).astype(jnp.bfloat16)
    spread = jnp.einsum("ikmn,iknp->imp", slabs, column_basis, preferred_element_type=jnp.float32)
    basis_wide = basis_vals.astype(jnp.float32)
    density_at = jnp.sum(basis_wide * spread, axis=(0, 1))
    scaled = (
        basis_wide * (weight_row.astype(jnp.float32) * potential(density_at))[None, None, :]
    ).astype(jnp.bfloat16)
    column_scaled = jnp.einsum(
        "ikj,jnp->iknp", matches, scaled, preferred_element_type=jnp.float32
    ).astype(jnp.bfloat16)
    return jnp.einsum(
        "imp,iknp->ikmn", basis_vals, column_scaled, preferred_element_type=jnp.float32
    )


def shards(density_blocks, neighbours, relevant, batch_count, basis_values, becke_weights):
    group_count = density_blocks.shape[0]
    reach = SPAN // 2
    arrived = []
    for offset, low_edge in ((1, group_count - reach), (-1, 0)):
        arrived.append(
            shifted(
                (
                    density_blocks[low_edge : low_edge + reach],
                    neighbours[low_edge : low_edge + reach],
                ),
                "grid",
                offset,
            )
        )
    before_blocks, before_lists = arrived[0]
    after_blocks, after_lists = arrived[1]
    window_blocks = jnp.concatenate([before_blocks, density_blocks, after_blocks], axis=0)
    window_lists = jnp.concatenate([before_lists, neighbours, after_lists], axis=0)
    window_base = lax.axis_index("grid") * group_count - reach
    loop_count = batch_count[0]
    source_groups, source_basis, source_weights = (relevant, basis_values, becke_weights)

    def visit(step_index, buffer):
        groups = source_groups[step_index]
        local_rows = groups - window_base
        blocks = batch_terms(
            window_blocks[local_rows],
            window_lists[local_rows],
            groups,
            source_basis[step_index],
            source_weights[step_index],
        )
        return buffer.at[local_rows].add(blocks)

    start_buffer = jnp.zeros((group_count + 2 * reach,) + density_blocks.shape[1:], jnp.float32)
    buffer = lax.fori_loop(0, loop_count, visit, start_buffer)
    halves = sum_at_owner(buffer, "rep", 1)
    owned_half = halves[reach : reach + group_count]
    gained = []
    for offset, low_edge in ((1, reach + group_count), (-1, 0)):
        gained.append(shifted(halves[low_edge : low_edge + reach], "grid", offset))
    owned_half = owned_half.at[:reach].add(gained[0])
    owned_half = owned_half.at[group_count - reach :].add(gained[1])
    return lax.all_gather(owned_half.astype(jnp.bfloat16), "rep", axis=1, tiled=True)


def solution(mesh):
    placed = (
        P("grid", None, None, None),
        P("grid", None),
        P(("grid", "rep"), None),
        P(("grid", "rep")),
        P(("grid", "rep"), None, None, None),
        P(("grid", "rep"), None),
    )
    return jax.shard_map(
        shards, mesh=mesh, in_specs=placed, out_specs=P("grid", None, None, None), check_vma=False
    )
```

profile of v0, /device:TPU:1, one launch (start us, length us, event | category | flops | bytes accessed | tf_op | source)
XLA Modules:
  0.0 335.1 jit_solution(412478288045447949)
XLA Ops:
  6.5 2.4 fusion.26
  9.0 4.1 %collective-permute-start.2 = (bf16[6,4,128,128]{3,2,1,0:T(8,128)(2,1)}, bf16[6,4,128,128]{3,2,1,0:T(8,128)(2,1)S(1)}, u32[]{:S(2)}, u32[]{:S(2)}) collective-permute-start(bf16[6,4,128,128]{3,2,1,0:T(8,128)(2,1)} %get-tuple-element.125), channel_id=1, source_target_pairs={{0,2},{2,4},{4,6},{6,8},{8,10},{10,12},{12,14},{14,16},{16,18},{18... | collective-permute-start | bytes 2359304 | tf_op jit(solution)/shard_map/ppermute | solution.py:13
  15.2 4.0 %collective-permute-start = (s32[6,4]{0,1:T(4,128)S(1)}, s32[6,4]{0,1:T(4,128)S(1)}, u32[]{:S(2)}, u32[]{:S(2)}) collective-permute-start(s32[6,4]{0,1:T(4,128)S(1)} %get-tuple-element.127), channel_id=1, source_target_pairs={{0,2},{2,4},{4,6},{6,8},{8,10},{10,12},{12,14},{14,16},{16,18},{18... | collective-permute-start | bytes 296 | tf_op jit(solution)/shard_map/ppermute | solution.py:13
  21.2 8.3 %collective-permute-done = s32[6,4]{0,1:T(4,128)S(1)} collective-permute-done((s32[6,4]{0,1:T(4,128)S(1)}, s32[6,4]{0,1:T(4,128)S(1)}, u32[]{:S(2)}, u32[]{:S(2)}) %collective-permute-start) | collective-permute-done | bytes 128 | tf_op jit(solution)/shard_map/ppermute | solution.py:13
  29.5 3.6 %collective-permute-done.1 = s32[6,4]{0,1:T(4,128)S(1)} collective-permute-done((s32[6,4]{0,1:T(4,128)S(1)}, s32[6,4]{0,1:T(4,128)S(1)}, u32[]{:S(2)}, u32[]{:S(2)}) %collective-permute-start.1) | collective-permute-done | bytes 128 | tf_op jit(solution)/shard_map/ppermute | solution.py:13
  34.0 5.0 %pad_maximum_fusion = bf16[40,4,128,128]{3,2,1,0:T(8,128)(2,1)} fusion(bf16[6,4,128,128]{3,2,1,0:T(8,128)(2,1)S(1)} %collective-permute-done.3, bf16[28,4,128,128]{3,2,1,0:T(8,128)(2,1)} %param.12, bf16[6,4,128,128]{3,2,1,0:T(8,128)(2,1)S(1)} %collective-permute-done.2), kind=kLoop, calls=%fused_computation.37 | loop fusion | flops 5242880 | bytes 10485760 | tf_op jit(solution)/shard_map/concatenate | solution.py:67
  39.0 5.3 %broadcast_in_dim.2 = f32[40,4,128,128]{3,2,1,0:T(8,128)} broadcast(f32[]{:T(128)} %constant.81.clone.1), dimensions={} | broadcast | bytes 10485764 | tf_op jit(solution)/shard_map/broadcast_in_dim | solution.py:85
  44.3 66.5 %while.12 = (s32[]{:T(128)}, f32[40,4,128,128]{3,2,1,0:T(8,128)}, s32[]{:T(128)}, s32[12,8]{1,0:T(8,128)S(1)}, s32[]{:T(128)}, /*index=5*/s32[40,4]{1,0:T(8,128)...) while((s32[]{:T(128)}, f32[40,4,128,128]{3,2,1,0:T(8,128)}, ...), condition=%wide.region_3.0_spmd, body=%wide.region_0.0_spmd.sunk | while | flops 287574176 | bytes 23076084 | solution.py:86
  46.7 3.2 gather_fusion
  56.3 4.4 %scatter_fusion = f32[40,4,128,128]{3,2,1,0:T(8,128)} fusion(f32[40,4,128,128]{3,2,1,0:T(8,128)} %get-tuple-element.198, s32[8]{0:T(128)S(1)} %fusion.47, f32[8,4,128,128]{3,2,1,0:T(8,128)S(1)} %copy.62), kind=kCustom, calls=%fused_computation.2.clone.1 | custom fusion | flops 524288 | bytes 6291488 | tf_op jit(solution)/shard_map/while/body/scatter-add | solution.py:83
  63.2 3.2 gather_fusion
  72.8 4.4 %scatter_fusion = f32[40,4,128,128]{3,2,1,0:T(8,128)} fusion(f32[40,4,128,128]{3,2,1,0:T(8,128)} %get-tuple-element.198, s32[8]{0:T(128)S(1)} %fusion.47, f32[8,4,128,128]{3,2,1,0:T(8,128)S(1)} %copy.62), kind=kCustom, calls=%fused_computation.2.clone.1 | custom fusion | flops 524288 | bytes 6291488 | tf_op jit(solution)/shard_map/while/body/scatter-add | solution.py:83
  79.7 3.2 gather_fusion
  89.3 4.4 %scatter_fusion = f32[40,4,128,128]{3,2,1,0:T(8,128)} fusion(f32[40,4,128,128]{3,2,1,0:T(8,128)} %get-tuple-element.198, s32[8]{0:T(128)S(1)} %fusion.47, f32[8,4,128,128]{3,2,1,0:T(8,128)S(1)} %copy.62), kind=kCustom, calls=%fused_computation.2.clone.1 | custom fusion | flops 524288 | bytes 6291488 | tf_op jit(solution)/shard_map/while/body/scatter-add | solution.py:83
  96.1 3.2 gather_fusion
  105.7 4.4 %scatter_fusion = f32[40,4,128,128]{3,2,1,0:T(8,128)} fusion(f32[40,4,128,128]{3,2,1,0:T(8,128)} %get-tuple-element.198, s32[8]{0:T(128)S(1)} %fusion.47, f32[8,4,128,128]{3,2,1,0:T(8,128)S(1)} %copy.62), kind=kCustom, calls=%fused_computation.2.clone.1 | custom fusion | flops 524288 | bytes 6291488 | tf_op jit(solution)/shard_map/while/body/scatter-add | solution.py:83
  110.8 4.8 %copy.23 = f32[2,40,2,128,128]{4,3,2,1,0:T(8,128)S(1)} copy(f32[2,40,2,128,128]{4,3,2,0,1:T(8,128)} %bitcast.73) | data formatting | bytes 20971520 | tf_op jit(solution)/shard_map/transpose | solution.py:18
  115.6 13.3 %all_to_all.5 = f32[2,40,2,128,128]{4,3,2,1,0:T(8,128)} all-to-all(f32[2,40,2,128,128]{4,3,2,1,0:T(8,128)S(1)} %copy.23), channel_id=1, replica_groups=mesh['grid'=128,'rep'=2] {'rep'}, dimensions={0} | all-to-all | bytes 20971520 | tf_op jit(solution)/shard_map/all_to_all | solution.py:23
  128.9 8.0 %reduce_sum.18 = f32[40,2,128,128]{3,2,1,0:T(8,128)} reduce(f32[2,40,2,128,128]{4,3,2,1,0:T(8,128)} %all_to_all.5, f32[]{:T(128)} %constant.81.clone.1), dimensions={0}, to_apply=%region_4.0 | reduce | flops 1310720 | bytes 15728644 | tf_op jit(solution)/shard_map/reduce_sum | solution.py:24
  138.5 3.3 collective-permute-start.4
  143.4 14.9 %collective-permute-done.4 = f32[6,2,128,128]{3,2,1,0:T(8,128)S(1)} collective-permute-done((f32[6,2,128,128]{3,2,1,0:T(8,128)S(1)}, f32[6,2,128,128]{3,2,1,0:T(8,128)S(1)}, u32[]{:S(2)}, u32[]{:S(2)}) %collective-permute-start.4) | collective-permute-done | bytes 786464 | tf_op jit(solution)/shard_map/ppermute | solution.py:13
  158.3 4.1 %collective-permute-done.5 = f32[6,2,128,128]{3,2,1,0:T(8,128)S(1)} collective-permute-done((f32[6,2,128,128]{3,2,1,0:T(8,128)S(1)}, f32[6,2,128,128]{3,2,1,0:T(8,128)S(1)}, u32[]{:S(2)}, u32[]{:S(2)}) %collective-permute-start.5) | collective-permute-done | bytes 786464 | tf_op jit(solution)/shard_map/ppermute | solution.py:13
  164.2 159.7 %all-gather.2.cloned.1.call-done = bf16[28,4,128,128]{3,2,1,0:T(8,128)(2,1)} async-done(((bf16[28,2,128,128]{3,2,1,0:T(8,128)(2,1)}), bf16[28,4,128,128]{3,2,1,0:T(8,128)(2,1)}) %all-gather.2.cloned.1.call-update) | async-done | bytes 3670032 | tf_op jit(solution)/shard_map/all_gather | solution.py:94
  323.8 4.4 %copy.73 = bf16[28,4,128,128]{3,2,1,0:T(8,128)(2,1)} copy(bf16[28,4,128,128]{3,2,1,0:T(8,128)(2,1)} %all-gather.2.cloned.1.call-done) | data formatting | bytes 7340032
  (71 shorter events, 42.4 us)
Async XLA Ops:
  6.5 317.3 %all-gather.2.cloned.1.call-start = ((), (), s32[]{:S(2)}) async-start(), calls=%async_computation.1 | async-start | bytes 5505024 | tf_op jit(solution)/shard_map/all_gather | solution.py:94
  9.0 25.0 %collective-permute-start.2 = (bf16[6,4,128,128]{3,2,1,0:T(8,128)(2,1)}, bf16[6,4,128,128]{3,2,1,0:T(8,128)(2,1)S(1)}, u32[]{:S(2)}, u32[]{:S(2)}) collective-permute-start(bf16[6,4,128,128]{3,2,1,0:T(8,128)(2,1)} %get-tuple-element.125), channel_id=1, source_target_pairs={{0,2},{2,4},{4,6},{6,8},{8,10},{10,12},{12,14},{14,16},{16,18},{18... | collective-permute-start | bytes 2359304 | tf_op jit(solution)/shard_map/ppermute | solution.py:13
  13.0 20.9 %collective-permute-start.3 = (bf16[6,4,128,128]{3,2,1,0:T(8,128)(2,1)S(1)}, bf16[6,4,128,128]{3,2,1,0:T(8,128)(2,1)S(1)}, u32[]{:S(2)}, u32[]{:S(2)}) collective-permute-start(bf16[6,4,128,128]{3,2,1,0:T(8,128)(2,1)S(1)} %get-tuple-element.126), channel_id=1, source_target_pairs={{2,0},{4,2},{6,4},{8,6},{10,8},{12,10},{14,12},{16,14},{18,16},{20... | collective-permute-start | bytes 2359304 | tf_op jit(solution)/shard_map/ppermute | solution.py:13
  15.2 14.3 %collective-permute-start = (s32[6,4]{0,1:T(4,128)S(1)}, s32[6,4]{0,1:T(4,128)S(1)}, u32[]{:S(2)}, u32[]{:S(2)}) collective-permute-start(s32[6,4]{0,1:T(4,128)S(1)} %get-tuple-element.127), channel_id=1, source_target_pairs={{0,2},{2,4},{4,6},{6,8},{8,10},{10,12},{12,14},{14,16},{16,18},{18... | collective-permute-start | bytes 296 | tf_op jit(solution)/shard_map/ppermute | solution.py:13
  19.1 14.0 %collective-permute-start.1 = (s32[6,4]{0,1:T(4,128)S(1)}, s32[6,4]{0,1:T(4,128)S(1)}, u32[]{:S(2)}, u32[]{:S(2)}) collective-permute-start(s32[6,4]{0,1:T(4,128)S(1)} %get-tuple-element.128), channel_id=1, source_target_pairs={{2,0},{4,2},{6,4},{8,6},{10,8},{12,10},{14,12},{16,14},{18,16},{20... | collective-permute-start | bytes 296 | tf_op jit(solution)/shard_map/ppermute | solution.py:13
  136.8 21.4 %copy-start = (f32[40,2,128,128]{3,2,1,0:T(8,128)S(1)}, f32[40,2,128,128]{3,2,1,0:T(8,128)}, u32[]{:S(2)}) copy-start(f32[40,2,128,128]{3,2,1,0:T(8,128)} %reduce_sum.18) | copy-start | bytes 15728644
  138.5 19.8 %collective-permute-start.4 = (f32[6,2,128,128]{3,2,1,0:T(8,128)S(1)}, f32[6,2,128,128]{3,2,1,0:T(8,128)S(1)}, u32[]{:S(2)}, u32[]{:S(2)}) collective-permute-start(f32[6,2,128,128]{3,2,1,0:T(8,128)S(1)} %get-tuple-element.124), channel_id=1, source_target_pairs={{0,2},{2,4},{4,6},{6,8},{8,10},{10,12},{12,14},{14,16},{16,18},{18... | collective-permute-start | bytes 2359304 | tf_op jit(solution)/shard_map/ppermute | solution.py:13
  141.8 16.5 %slice-start = ((f32[40,2,128,128]{3,2,1,0:T(8,128)}), f32[28,2,128,128]{3,2,1,0:T(8,128)S(1)}, s32[]{:S(2)}) async-start(f32[40,2,128,128]{3,2,1,0:T(8,128)} %reduce_sum.18), calls=%async_computation.2 | async-start | bytes 7340032 | tf_op jit(solution)/shard_map/slice | solution.py:88
  141.8 20.6 %collective-permute-start.5 = (f32[6,2,128,128]{3,2,1,0:T(8,128)S(1)}, f32[6,2,128,128]{3,2,1,0:T(8,128)S(1)}, u32[]{:S(2)}, u32[]{:S(2)}) collective-permute-start(f32[6,2,128,128]{3,2,1,0:T(8,128)S(1)} %get-tuple-element.123), channel_id=1, source_target_pairs={{2,0},{4,2},{6,4},{8,6},{10,8},{12,10},{14,12},{16,14},{18,16},{20... | collective-permute-start | bytes 2359304 | tf_op jit(solution)/shard_map/ppermute | solution.py:13
Sparse Core Ops, SparseCore 0:
  164.3 159.5 all-gather.1
where the time goes:
time: 337 us; the launch traced here: 335 us
  waiting for transfers between devices  191 us (57%)
  local copies, waits for them, and re-layouts  47.8 us (14%)
  other arithmetic  37.7 us (11%)
  starting transfers between devices  15.5 us (5%)
  between operations  13.5 us (4%)
  blocking collectives  13.3 us (4%)
  matrix products  13.2 us (4%)
  loops' own time  3.61 us (1%)
    all_gather x1, waiting for transfers between devices, shards(): lax.all_gather(owned_half.astype(jnp.bfloat16), 'rep', axis=1, tiled=True)  160 us
    ppermute x6, waiting for transfers between devices, shifted(): return lax.ppermute(block, axis, route)  30.8 us
    scatter-add x4, other arithmetic, visit(): return buffer.at[local_rows].add(blocks)  17.6 us
    ppermute x6, starting transfers between devices, shifted(): return lax.ppermute(block, axis, route)  15.5 us
    all_to_all x1, blocking collectives, sum_at_owner(): lax.all_to_all(in_blocks(array, dim, count), axis, 0, 0, tiled=True)  13.3 us
    gather x4, local copies, waits for them, and re-layouts, visit(): window_blocks[local_rows]  12.9 us
    reduce_sum x1, other arithmetic, sum_at_owner(): return jnp.sum(pieces, axis=0)  7.96 us
    transpose x4, local copies, waits for them, and re-layouts, batch_terms(): jnp.einsum('imp,iknp->ikmn', basis_vals, column_scaled, preferred_element...  7.67 us
  transfers between devices with their start and end apart: 7, of which 5 were waited for; matrix products, arithmetic and copies ran while one was open for 1% of the time, Pallas kernels for 0%

commit v1 on v0

--- a/solution.py
+++ b/solution.py
@@ -5,6 +5,11 @@
 
 SPAN = 12
 slater_coef = 0.9847450218426965
+
+
+def swapped_in(x, name, d):
+    stack = jnp.stack([x] * lax.axis_size(name))
+    return jnp.concatenate(lax.all_to_all(stack, name, 0, 0), axis=d)
 
 
 def shifted(block, axis, distance):
@@ -91,7 +96,7 @@
         gained.append(shifted(halves[low_edge : low_edge + reach], "grid", offset))
     owned_half = owned_half.at[:reach].add(gained[0])
     owned_half = owned_half.at[group_count - reach :].add(gained[1])
-    return lax.all_gather(owned_half.astype(jnp.bfloat16), "rep", axis=1, tiled=True)
+    return swapped_in(owned_half.astype(jnp.bfloat16), "rep", 1)
 
 
 def solution(mesh):

time: 337 us -> 308 us (0.914)
  the two profiles are of different devices: /device:TPU:1 before, /device:TPU:123 now
where the time goes in v1:
time: 308 us; the launch traced here: 306 us
  blocking collectives  171 us (56%)
  local copies, waits for them, and re-layouts  38.8 us (13%)
  waiting for transfers between devices  31.7 us (10%)
  other arithmetic  31.3 us (10%)
  starting transfers between devices  20.6 us (7%)
  matrix products  9.89 us (3%)
    all_to_all x1, blocking collectives, sum_at_owner(): lax.all_to_all(in_blocks(array, dim, count), axis, 0, 0, tiled=True)  163 us
    ppermute x6, waiting for transfers between devices, shifted(): return lax.ppermute(block, axis, route)  31.7 us
    ppermute x6, starting transfers between devices, shifted(): return lax.ppermute(block, axis, route)  20.6 us
    scatter-add x3, other arithmetic, visit(): return buffer.at[local_rows].add(blocks)  13.2 us
    gather x3, local copies, waits for them, and re-layouts, visit(): window_blocks[local_rows]  9.7 us
    reduce_sum x1, other arithmetic, sum_at_owner(): return jnp.sum(pieces, axis=0)  7.95 us
    all_to_all x1, blocking collectives, swapped_in(): return jnp.concatenate(lax.all_to_all(stack, name, 0, 0), axis=d)  7.54 us
  transfers between devices with their start and end apart: 6, of which 4 were waited for; matrix products, arithmetic and copies ran while one was open for 1% of the time, Pallas kernels for 0%

profile of v1, /device:TPU:123, one launch (start us, length us, event | category | flops | bytes accessed | tf_op | source)
XLA Modules:
  0.0 305.9 jit_solution(1316232481326029158)
XLA Ops:
  0.0 2.4 fusion.26
  2.4 4.4 %collective-permute-start.2 = (bf16[6,4,128,128]{3,2,1,0:T(8,128)(2,1)}, bf16[6,4,128,128]{3,2,1,0:T(8,128)(2,1)S(1)}, u32[]{:S(2)}, u32[]{:S(2)}) collective-permute-start(bf16[6,4,128,128]{3,2,1,0:T(8,128)(2,1)} %get-tuple-element.125), channel_id=1, source_target_pairs={{0,2},{2,4},{4,6},{6,8},{8,10},{10,12},{12,14},{14,16},{16,18},{18... | collective-permute-start | bytes 2359304 | tf_op jit(solution)/shard_map/ppermute | solution.py:18
  6.8 1.9 collective-permute-start.3
  9.6 6.7 %collective-permute-start = (s32[6,4]{0,1:T(4,128)S(1)}, s32[6,4]{0,1:T(4,128)S(1)}, u32[]{:S(2)}, u32[]{:S(2)}) collective-permute-start(s32[6,4]{0,1:T(4,128)S(1)} %get-tuple-element.127), channel_id=1, source_target_pairs={{0,2},{2,4},{4,6},{6,8},{8,10},{10,12},{12,14},{14,16},{16,18},{18... | collective-permute-start | bytes 296 | tf_op jit(solution)/shard_map/ppermute | solution.py:18
  19.0 4.4 %collective-permute-done = s32[6,4]{0,1:T(4,128)S(1)} collective-permute-done((s32[6,4]{0,1:T(4,128)S(1)}, s32[6,4]{0,1:T(4,128)S(1)}, u32[]{:S(2)}, u32[]{:S(2)}) %collective-permute-start) | collective-permute-done | bytes 128 | tf_op jit(solution)/shard_map/ppermute | solution.py:18
  23.4 6.9 %collective-permute-done.1 = s32[6,4]{0,1:T(4,128)S(1)} collective-permute-done((s32[6,4]{0,1:T(4,128)S(1)}, s32[6,4]{0,1:T(4,128)S(1)}, u32[]{:S(2)}, u32[]{:S(2)}) %collective-permute-start.1) | collective-permute-done | bytes 128 | tf_op jit(solution)/shard_map/ppermute | solution.py:18
  31.1 5.0 %pad_maximum_fusion = bf16[40,4,128,128]{3,2,1,0:T(8,128)(2,1)} fusion(bf16[6,4,128,128]{3,2,1,0:T(8,128)(2,1)S(1)} %collective-permute-done.3, bf16[28,4,128,128]{3,2,1,0:T(8,128)(2,1)} %param.12, bf16[6,4,128,128]{3,2,1,0:T(8,128)(2,1)S(1)} %collective-permute-done.2), kind=kLoop, calls=%fused_computation.37 | loop fusion | flops 5242880 | bytes 10485760 | tf_op jit(solution)/shard_map/concatenate | solution.py:72
  36.1 5.3 %broadcast_in_dim.2 = f32[40,4,128,128]{3,2,1,0:T(8,128)} broadcast(f32[]{:T(128)} %constant.81.clone.1), dimensions={} | broadcast | bytes 10485764 | tf_op jit(solution)/shard_map/broadcast_in_dim | solution.py:90
  41.4 50.0 %while.12 = (s32[]{:T(128)}, f32[40,4,128,128]{3,2,1,0:T(8,128)}, s32[]{:T(128)}, s32[12,8]{1,0:T(8,128)S(1)}, s32[]{:T(128)}, /*index=5*/s32[40,4]{1,0:T(8,128)...) while((s32[]{:T(128)}, f32[40,4,128,128]{3,2,1,0:T(8,128)}, ...), condition=%wide.region_3.0_spmd, body=%wide.region_0.0_spmd.sunk | while | flops 287574176 | bytes 23076084 | solution.py:91
  43.9 3.2 %gather_fusion = bf16[8,4,128,128]{3,2,1,0:T(8,128)(2,1)S(1)} fusion(bf16[40,4,128,128]{3,2,1,0:T(8,128)(2,1)} %get-tuple-element.217, s32[1024]{0:T(1024)S(1)} %pad_clamp_fusion.2), kind=kCustom, calls=%fused_computation.1.clone.1 | custom fusion | bytes 2097184 | tf_op jit(solution)/shard_map/while/body/gather | solution.py:82
  53.5 4.4 %scatter_fusion = f32[40,4,128,128]{3,2,1,0:T(8,128)} fusion(f32[40,4,128,128]{3,2,1,0:T(8,128)} %get-tuple-element.198, s32[8]{0:T(128)S(1)} %fusion.47, f32[8,4,128,128]{3,2,1,0:T(8,128)S(1)} %copy.63), kind=kCustom, calls=%fused_computation.2.clone.1 | custom fusion | flops 524288 | bytes 6291488 | tf_op jit(solution)/shard_map/while/body/scatter-add | solution.py:88
  60.3 3.2 %gather_fusion = bf16[8,4,128,128]{3,2,1,0:T(8,128)(2,1)S(1)} fusion(bf16[40,4,128,128]{3,2,1,0:T(8,128)(2,1)} %get-tuple-element.217, s32[1024]{0:T(1024)S(1)} %pad_clamp_fusion.2), kind=kCustom, calls=%fused_computation.1.clone.1 | custom fusion | bytes 2097184 | tf_op jit(solution)/shard_map/while/body/gather | solution.py:82
  69.9 4.4 %scatter_fusion = f32[40,4,128,128]{3,2,1,0:T(8,128)} fusion(f32[40,4,128,128]{3,2,1,0:T(8,128)} %get-tuple-element.198, s32[8]{0:T(128)S(1)} %fusion.47, f32[8,4,128,128]{3,2,1,0:T(8,128)S(1)} %copy.63), kind=kCustom, calls=%fused_computation.2.clone.1 | custom fusion | flops 524288 | bytes 6291488 | tf_op jit(solution)/shard_map/while/body/scatter-add | solution.py:88
  76.8 3.2 %gather_fusion = bf16[8,4,128,128]{3,2,1,0:T(8,128)(2,1)S(1)} fusion(bf16[40,4,128,128]{3,2,1,0:T(8,128)(2,1)} %get-tuple-element.217, s32[1024]{0:T(1024)S(1)} %pad_clamp_fusion.2), kind=kCustom, calls=%fused_computation.1.clone.1 | custom fusion | bytes 2097184 | tf_op jit(solution)/shard_map/while/body/gather | solution.py:82
  86.4 4.4 %scatter_fusion = f32[40,4,128,128]{3,2,1,0:T(8,128)} fusion(f32[40,4,128,128]{3,2,1,0:T(8,128)} %get-tuple-element.198, s32[8]{0:T(128)S(1)} %fusion.47, f32[8,4,128,128]{3,2,1,0:T(8,128)S(1)} %copy.63), kind=kCustom, calls=%fused_computation.2.clone.1 | custom fusion | flops 524288 | bytes 6291488 | tf_op jit(solution)/shard_map/while/body/scatter-add | solution.py:88
  91.4 4.8 %copy.23 = f32[2,40,2,128,128]{4,3,2,1,0:T(8,128)S(1)} copy(f32[2,40,2,128,128]{4,3,2,0,1:T(8,128)} %bitcast.78) | data formatting | bytes 20971520 | tf_op jit(solution)/shard_map/transpose | solution.py:23
  96.3 163.1 %all_to_all.10 = f32[2,40,2,128,128]{4,3,2,1,0:T(8,128)} all-to-all(f32[2,40,2,128,128]{4,3,2,1,0:T(8,128)S(1)} %copy.23), channel_id=1, replica_groups=mesh['grid'=128,'rep'=2] {'rep'}, dimensions={0} | all-to-all | bytes 20971520 | tf_op jit(solution)/shard_map/all_to_all | solution.py:28
  259.4 8.0 %reduce_sum.18 = f32[40,2,128,128]{3,2,1,0:T(8,128)} reduce(f32[2,40,2,128,128]{4,3,2,1,0:T(8,128)} %all_to_all.10, f32[]{:T(128)} %constant.81.clone.1), dimensions={0}, to_apply=%region_4.0 | reduce | flops 1310720 | bytes 15728644 | tf_op jit(solution)/shard_map/reduce_sum | solution.py:29
  269.0 2.1 collective-permute-start.4
  271.1 3.6 %collective-permute-start.5 = (f32[6,2,128,128]{3,2,1,0:T(8,128)S(1)}, f32[6,2,128,128]{3,2,1,0:T(8,128)S(1)}, u32[]{:S(2)}, u32[]{:S(2)}) collective-permute-start(f32[6,2,128,128]{3,2,1,0:T(8,128)S(1)} %get-tuple-element.123), channel_id=1, source_target_pairs={{2,0},{4,2},{6,4},{8,6},{10,8},{12,10},{14,12},{16,14},{18,16},{20... | collective-permute-start | bytes 2359304 | tf_op jit(solution)/shard_map/ppermute | solution.py:18
  274.7 15.0 %collective-permute-done.4 = f32[6,2,128,128]{3,2,1,0:T(8,128)S(1)} collective-permute-done((f32[6,2,128,128]{3,2,1,0:T(8,128)S(1)}, f32[6,2,128,128]{3,2,1,0:T(8,128)S(1)}, u32[]{:S(2)}, u32[]{:S(2)}) %collective-permute-start.4) | collective-permute-done | bytes 786464 | tf_op jit(solution)/shard_map/ppermute | solution.py:18
  289.8 5.4 %collective-permute-done.5 = f32[6,2,128,128]{3,2,1,0:T(8,128)S(1)} collective-permute-done((f32[6,2,128,128]{3,2,1,0:T(8,128)S(1)}, f32[6,2,128,128]{3,2,1,0:T(8,128)S(1)}, u32[]{:S(2)}, u32[]{:S(2)}) %collective-permute-start.5) | collective-permute-done | bytes 786464 | tf_op jit(solution)/shard_map/ppermute | solution.py:18
  296.1 7.5 %all_to_all.11 = bf16[2,28,2,128,128]{4,3,2,1,0:T(8,128)(2,1)S(1)} all-to-all(bf16[2,28,2,128,128]{4,3,2,1,0:T(8,128)(2,1)S(1)} %pad_maximum_fusion.1), channel_id=1, replica_groups=mesh['grid'=128,'rep'=2] {'rep'}, dimensions={0} | all-to-all | bytes 7340032 | tf_op jit(solution)/shard_map/all_to_all | solution.py:12
  303.6 2.3 copy.24
  (55 shorter events, 31.2 us)
Async XLA Ops:
  2.4 28.7 %collective-permute-start.2 = (bf16[6,4,128,128]{3,2,1,0:T(8,128)(2,1)}, bf16[6,4,128,128]{3,2,1,0:T(8,128)(2,1)S(1)}, u32[]{:S(2)}, u32[]{:S(2)}) collective-permute-start(bf16[6,4,128,128]{3,2,1,0:T(8,128)(2,1)} %get-tuple-element.125), channel_id=1, source_target_pairs={{0,2},{2,4},{4,6},{6,8},{8,10},{10,12},{12,14},{14,16},{16,18},{18... | collective-permute-start | bytes 2359304 | tf_op jit(solution)/shard_map/ppermute | solution.py:18
  6.8 24.3 %collective-permute-start.3 = (bf16[6,4,128,128]{3,2,1,0:T(8,128)(2,1)S(1)}, bf16[6,4,128,128]{3,2,1,0:T(8,128)(2,1)S(1)}, u32[]{:S(2)}, u32[]{:S(2)}) collective-permute-start(bf16[6,4,128,128]{3,2,1,0:T(8,128)(2,1)S(1)} %get-tuple-element.126), channel_id=1, source_target_pairs={{2,0},{4,2},{6,4},{8,6},{10,8},{12,10},{14,12},{16,14},{18,16},{20... | collective-permute-start | bytes 2359304 | tf_op jit(solution)/shard_map/ppermute | solution.py:18
  9.6 13.8 %collective-permute-start = (s32[6,4]{0,1:T(4,128)S(1)}, s32[6,4]{0,1:T(4,128)S(1)}, u32[]{:S(2)}, u32[]{:S(2)}) collective-permute-start(s32[6,4]{0,1:T(4,128)S(1)} %get-tuple-element.127), channel_id=1, source_target_pairs={{0,2},{2,4},{4,6},{6,8},{8,10},{10,12},{12,14},{14,16},{16,18},{18... | collective-permute-start | bytes 296 | tf_op jit(solution)/shard_map/ppermute | solution.py:18
  16.3 14.0 %collective-permute-start.1 = (s32[6,4]{0,1:T(4,128)S(1)}, s32[6,4]{0,1:T(4,128)S(1)}, u32[]{:S(2)}, u32[]{:S(2)}) collective-permute-start(s32[6,4]{0,1:T(4,128)S(1)} %get-tuple-element.128), channel_id=1, source_target_pairs={{2,0},{4,2},{6,4},{8,6},{10,8},{12,10},{14,12},{16,14},{18,16},{20... | collective-permute-start | bytes 296 | tf_op jit(solution)/shard_map/ppermute | solution.py:18
  267.3 22.4 %copy-start = (f32[40,2,128,128]{3,2,1,0:T(8,128)S(1)}, f32[40,2,128,128]{3,2,1,0:T(8,128)}, u32[]{:S(2)}) copy-start(f32[40,2,128,128]{3,2,1,0:T(8,128)} %reduce_sum.18) | copy-start | bytes 15728644
  269.0 20.8 %collective-permute-start.4 = (f32[6,2,128,128]{3,2,1,0:T(8,128)S(1)}, f32[6,2,128,128]{3,2,1,0:T(8,128)S(1)}, u32[]{:S(2)}, u32[]{:S(2)}) collective-permute-start(f32[6,2,128,128]{3,2,1,0:T(8,128)S(1)} %get-tuple-element.124), channel_id=1, source_target_pairs={{0,2},{2,4},{4,6},{6,8},{8,10},{10,12},{12,14},{14,16},{16,18},{18... | collective-permute-start | bytes 2359304 | tf_op jit(solution)/shard_map/ppermute | solution.py:18
  271.0 18.7 %slice-start = ((f32[40,2,128,128]{3,2,1,0:T(8,128)}), f32[28,2,128,128]{3,2,1,0:T(8,128)S(1)}, s32[]{:S(2)}) async-start(f32[40,2,128,128]{3,2,1,0:T(8,128)} %reduce_sum.18), calls=%async_computation.2 | async-start | bytes 7340032 | tf_op jit(solution)/shard_map/slice | solution.py:93
  271.1 24.2 %collective-permute-start.5 = (f32[6,2,128,128]{3,2,1,0:T(8,128)S(1)}, f32[6,2,128,128]{3,2,1,0:T(8,128)S(1)}, u32[]{:S(2)}, u32[]{:S(2)}) collective-permute-start(f32[6,2,128,128]{3,2,1,0:T(8,128)S(1)} %get-tuple-element.123), channel_id=1, source_target_pairs={{2,0},{4,2},{6,4},{8,6},{10,8},{12,10},{14,12},{16,14},{18,16},{20... | collective-permute-start | bytes 2359304 | tf_op jit(solution)/shard_map/ppermute | solution.py:18
